TPU v7x, 32 devices: a whole 2x2x4 slice. The times are simulated.
32 devices in a mesh: seq: 8 (over z, y), tp: 4 (over x, core).
Axes of the slice: x: 2, y: 2, z: 4, core: 2. Of those that a mesh axis runs over, the one named last changes fastest.
Arguments:
- prefill_tokens: bfloat16 [4096, 2304], P('seq'), may hold values from -6 to 6
- decode_tokens: bfloat16 [64, 2304], P('seq'), may hold values from -6 to 6
- attention_gain: float32 [2304], replicated, may hold values from 0.5 to 1.5
- qkv_weight: bfloat16 [2304, 3, 2304], P(None, None, 'tp'), may hold values from -0.125 to 0.125
- out_weight: bfloat16 [2304, 2304], P('tp'), may hold values from -0.375 to 0.375
- feedforward_gain: float32 [2304], replicated, may hold values from 0.5 to 1.5
- prefill_cache: bfloat16 [8, 2, 1024, 2304], P('seq', None, None, 'tp'), may hold values from -420 to 420
- prefill_offsets: int32 [8], P('seq'), may hold values from 0 to 1024, as said below
- decode_cache: bfloat16 [64, 2, 256, 2304], P('seq', None, None, 'tp'), may hold values from -420 to 420
- decode_lengths: int32 [64], P('seq'), may hold values from 1 to 256, as said below
- request_slot: int32 [64], replicated, may hold values from 0 to 63, each once
Outputs:
- prefill_hidden: bfloat16 [4096, 2304], P('seq')
- decode_hidden: bfloat16 [64, 2304], P('seq')
- prefill_normed: bfloat16 [4096, 2304], P('seq')
- decode_normed: bfloat16 [64, 2304], P('seq')
Inputs may be any that keep to these rules, and one draw needn't show every extreme that they name: `request_slot`: each slot is named by exactly one request. `decode_lengths`: some slot holds exactly 256 positions. `prefill_offsets`: some request has exactly 1024 cached positions.
All inputs are finite; a program needn't handle non-finite values.
Results may differ from a plain program's by a relative error of at most 0.014.
The roundings to bfloat16 on the way count: a program that leaves them out, or rounds other values in their place, can miss the bound.
Values may be sent and summed in bfloat16 or wider, within the bound.
A program may use at most 128 MiB of HBM per device.

v0:
```python
import math
import jax
import jax.numpy as jnp
from jax import lax
from jax.sharding import PartitionSpec as P

HEAD = 64
RMS_EPSILON = 1e-05
ROPE_BASE = 10000.0
NEGATIVE = -1e30


def rms_norm(stream, gain):
    widened = stream.astype(jnp.float32)
    inverse = lax.rsqrt(jnp.mean(widened * widened, axis=-1, keepdims=True) + RMS_EPSILON)
    return widened * inverse * gain


def rotate(vectors, positions):
    half_dim = vectors.shape[-1] // 2
    exponent = jnp.arange(half_dim, dtype=jnp.float32) * (2.0 / vectors.shape[-1])
    frequency = ROPE_BASE ** (-exponent)
    angles = positions[:, None] * frequency[None, :]
    cosine = jnp.cos(angles)[:, None, :]
    sine_part = jnp.sin(angles)[:, None, :]
    first_half = vectors[..., :half_dim]
    second_half = vectors[..., half_dim:]
    return jnp.concatenate(
        [
            first_half * cosine - second_half * sine_part,
            second_half * cosine + first_half * sine_part,
        ],
        axis=-1,
    )


def prefill_attention(block_rows, cache_pair, offset, head_count):
    span_rows = block_rows.shape[0]
    cache_len = cache_pair.shape[1]
    score_scale = 1.0 / math.sqrt(HEAD)
    positions = offset.astype(jnp.float32) + jnp.arange(span_rows, dtype=jnp.float32)
    queries = rotate(
        block_rows[:, 0].reshape(span_rows, head_count, HEAD).astype(jnp.float32), positions
    ).astype(jnp.bfloat16)
    new_keys = rotate(
        block_rows[:, 1].reshape(span_rows, head_count, HEAD).astype(jnp.float32), positions
    ).astype(jnp.bfloat16)
    new_values = block_rows[:, 2].reshape(span_rows, head_count, HEAD)
    cache_keys = cache_pair[0].reshape(cache_len, head_count, HEAD)
    cache_values = cache_pair[1].reshape(cache_len, head_count, HEAD)
    cache_scores = (
        jnp.einsum("qhe,khe->hqk", queries, cache_keys, preferred_element_type=jnp.float32)
        * score_scale
    )
    span_scores = (
        jnp.einsum("qhe,khe->hqk", queries, new_keys, preferred_element_type=jnp.float32)
        * score_scale
    )
    cache_visible = (jnp.arange(cache_len, dtype=jnp.int32) < offset)[None, None, :]
    causal = (
        jnp.arange(span_rows, dtype=jnp.int32)[None, :]
        <= jnp.arange(span_rows, dtype=jnp.int32)[:, None]
    )[None]
    cache_scores = jnp.where(cache_visible, cache_scores, NEGATIVE)
    span_scores = jnp.where(causal, span_scores, NEGATIVE)
    row_peak = jnp.maximum(
        jnp.max(cache_scores, axis=-1, keepdims=True), jnp.max(span_scores, axis=-1, keepdims=True)
    )
    cache_exp = jnp.exp(cache_scores - row_peak)
    span_exp = jnp.exp(span_scores - row_peak)
    denominator = jnp.sum(cache_exp, axis=-1, keepdims=True) + jnp.sum(
        span_exp, axis=-1, keepdims=True
    )
    cache_weights = (cache_exp / denominator).astype(jnp.bfloat16)
    span_weights = (span_exp / denominator).astype(jnp.bfloat16)
    attended = jnp.einsum(
        "hqk,khe->qhe", cache_weights, cache_values, preferred_element_type=jnp.float32
    )
    attended = attended + jnp.einsum(
        "hqk,khe->qhe", span_weights, new_values, preferred_element_type=jnp.float32
    )
    return attended.reshape(span_rows, head_count * HEAD).astype(jnp.bfloat16)


def decode_attention(routed, cache_block, lengths, head_count):
    slot_count = routed.shape[0]
    cache_len = cache_block.shape[2]
    score_scale = 1.0 / math.sqrt(HEAD)
    positions = lengths.astype(jnp.float32)
    queries = rotate(
        routed[:, 0].reshape(slot_count, head_count, HEAD).astype(jnp.float32), positions
    ).astype(jnp.bfloat16)
    new_keys = rotate(
        routed[:, 1].reshape(slot_count, head_count, HEAD).astype(jnp.float32), positions
    ).astype(jnp.bfloat16)
    new_values = routed[:, 2].reshape(slot_count, head_count, HEAD)
    cache_keys = cache_block[:, 0].reshape(slot_count, cache_len, head_count, HEAD)
    cache_values = cache_block[:, 1].reshape(slot_count, cache_len, head_count, HEAD)
    cache_scores = (
        jnp.einsum("she,skhe->shk", queries, cache_keys, preferred_element_type=jnp.float32)
        * score_scale
    )
    self_scores = (
        jnp.einsum("she,she->sh", queries, new_keys, preferred_element_type=jnp.float32)
        * score_scale
    )
    visible = (jnp.arange(cache_len, dtype=jnp.int32)[None, :] < lengths[:, None])[:, None, :]
    cache_scores = jnp.where(visible, cache_scores, NEGATIVE)
    row_peak = jnp.maximum(jnp.max(cache_scores, axis=-1), self_scores)
    cache_exp = jnp.exp(cache_scores - row_peak[..., None])
    self_exp = jnp.exp(self_scores - row_peak)
    denominator = jnp.sum(cache_exp, axis=-1) + self_exp
    cache_weights = (cache_exp / denominator[..., None]).astype(jnp.bfloat16)
    self_weights = (self_exp / denominator).astype(jnp.bfloat16)
    attended = jnp.einsum(
        "shk,skhe->she", cache_weights, cache_values, preferred_element_type=jnp.float32
    )
    attended = attended + self_weights.astype(jnp.float32)[..., None] * new_values.astype(
        jnp.float32
    )
    return attended.reshape(slot_count, head_count * HEAD).astype(jnp.bfloat16)


def local(
    prefill_tokens,
    decode_tokens,
    attention_gain,
    qkv_weight,
    out_weight,
    feedforward_gain,
    prefill_cache,
    prefill_offsets,
    decode_cache,
    decode_lengths,
    request_slot,
):
    span_rows = prefill_tokens.shape[0]
    decode_rows = decode_tokens.shape[0]
    model_width = prefill_tokens.shape[1]
    local_width = out_weight.shape[0]
    head_count = local_width // HEAD
    tokens_all = jnp.concatenate([prefill_tokens, decode_tokens], axis=0)
    normed_in = rms_norm(tokens_all, attention_gain).astype(jnp.bfloat16)
    projected = jnp.dot(
        normed_in,
        qkv_weight.reshape(model_width, 3 * local_width),
        preferred_element_type=jnp.float32,
    ).astype(jnp.bfloat16)
    projected = projected.reshape(-1, 3, local_width)
    prefill_block = projected[:span_rows]
    decode_block = projected[span_rows:]
    seq_rank = lax.axis_index("seq")
    own_slots = seq_rank * decode_rows + jnp.arange(decode_rows, dtype=jnp.int32)
    arrived = lax.all_gather(decode_block, "seq", axis=0, tiled=True)
    picker = (request_slot[None, :] == own_slots[:, None]).astype(jnp.bfloat16)
    routed = jnp.einsum("sr,rcw->scw", picker, arrived, preferred_element_type=jnp.float32).astype(
        jnp.bfloat16
    )
    slot_results = decode_attention(routed, decode_cache, decode_lengths, head_count)
    prefill_attended = prefill_attention(
        prefill_block, prefill_cache[0], prefill_offsets[0], head_count
    )
    my_slots = lax.dynamic_slice_in_dim(request_slot, seq_rank * decode_rows, decode_rows)
    shard_piece = lax.all_gather(slot_results, "seq", axis=0, tiled=True)
    slot_ids = jnp.arange(shard_piece.shape[0], dtype=jnp.int32)
    picker = (my_slots[:, None] == slot_ids[None, :]).astype(jnp.bfloat16)
    returned = jnp.dot(picker, shard_piece, preferred_element_type=jnp.float32).astype(jnp.bfloat16)
    attended_all = jnp.concatenate([prefill_attended, returned], axis=0)
    partial_value = jnp.dot(attended_all, out_weight, preferred_element_type=jnp.float32)
    combined = lax.psum(partial_value.astype(jnp.bfloat16), "tp").astype(jnp.float32)
    hidden = (tokens_all.astype(jnp.float32) + combined).astype(jnp.bfloat16)
    normed = rms_norm(hidden, feedforward_gain).astype(jnp.bfloat16)
    return (hidden[:span_rows], hidden[span_rows:], normed[:span_rows], normed[span_rows:])


def solution(mesh):
    placed = (
        P("seq", None),
        P("seq", None),
        P(),
        P(None, None, "tp"),
        P("tp", None),
        P(),
        P("seq", None, None, "tp"),
        P("seq"),
        P("seq", None, None, "tp"),
        P("seq"),
        P(),
    )
    return jax.shard_map(
        local,
        mesh=mesh,
        in_specs=placed,
        out_specs=(P("seq", None), P("seq", None), P("seq", None), P("seq", None)),
        check_vma=False,
    )
```

profile of v0, /device:TPU:0, one launch (start us, length us, event | category | flops | bytes accessed | tf_op | source)
XLA Modules:
  0.0 215.5 jit_solution(18062923695454391334)
XLA Ops:
  8.8 2.4 %fusion.8 = f32[520]{0:T(1024)S(1)} fusion(bf16[8,2304]{1,0:T(8,128)(2,1)} %param.12, bf16[512,2304]{1,0:T(8,128)(2,1)} %param.11), kind=kLoop, calls=%fused_computation.19 | loop fusion | flops 7187960 | bytes 2398240 | tf_op jit(solution)/shard_map/reduce_sum | solution.py:15
  11.2 8.6 %convolution_convert_fusion.1 = bf16[520,1728]{1,0:T(8,128)(2,1)S(1)} fusion(bf16[2304,1728]{0,1:T(8,128)(2,1)} %bitcast.71, f32[2304]{0:T(1024)} %param.13, f32[520]{0:T(1024)S(1)} %add_rsqrt_fusion.1, bf16[8,2304]{1,0:T(8,128)(2,1)} %param.12, bf16[512,2304]{1,0:T(8,128)(2,1)} %param.11), kind=kOutput, calls=%fused_computation.25 | convolution fusion | flops 4149849600 | bytes 12167200 | tf_op jit(solution)/shard_map/dot_general | solution.py:144
  19.8 1.4 slice.106
  21.3 2.5 %fusion.55 = (bf16[8,1,256,576]{2,3,1,0:T(8,128)(2,1)}, bf16[8,1,256,576]{2,3,1,0:T(8,128)(2,1)}) fusion(bf16[8,2,256,576]{2,3,1,0:T(8,128)(2,1)S(1)} %bitcast.64), kind=kLoop, calls=%fused_computation.103 | loop fusion | bytes 9437184 | tf_op jit(solution)/shard_map/slice | solution.py:97
  23.9 32.5 %all_gather.6 = bf16[64,3,576]{2,0,1:T(8,128)(2,1)S(1)} all-gather(bf16[8,3,576]{2,0,1:T(8,128)(2,1)S(1)} %copy.25), channel_id=1, replica_groups=mesh['seq'=8,'tp'=4] {'seq'}, dimensions={0}, use_global_device_ids=true | all-gather | bytes 248832 | tf_op jit(solution)/shard_map/all_gather | solution.py:154
  57.4 2.1 fusion.35
  60.1 2.4 %fusion.29 = f32[8,9,1,64]{3,2,1,0:T(1,128)S(1)} fusion(bf16[8,256,9,64]{1,3,2,0:T(8,128)(2,1)} %bitcast.68, bf16[8,9,256,1]{2,0,1,3:T(8,128)(2,1)S(1)} %fusion.37), kind=kOutput, calls=%fused_computation.53 | convolution fusion | flops 2359296 | bytes 2414592 | tf_op jit(solution)/shard_map/shk,skhe->she/dot_general | solution.py:115
  62.6 30.5 %all_gather.7 = bf16[64,576]{1,0:T(8,128)(2,1)S(1)} all-gather(bf16[8,576]{1,0:T(8,128)(2,1)S(1)} %convert_element_type.124), channel_id=1, replica_groups=mesh['seq'=8,'tp'=4] {'seq'}, dimensions={0}, use_global_device_ids=true | all-gather | bytes 82944 | tf_op jit(solution)/shard_map/all_gather | solution.py:164
  94.2 3.2 %fusion.56 = (bf16[1,1,1024,576]{2,3,1,0:T(8,128)(2,1)}, bf16[1,1,1024,576]{2,3,1,0:T(8,128)(2,1)}) fusion(bf16[1,2,1024,576]{2,3,1,0:T(8,128)(2,1)} %param.17), kind=kLoop, calls=%fused_computation.104 | loop fusion | bytes 4718592 | tf_op jit(solution)/shard_map/slice | solution.py:49
  98.1 4.0 %copy.23 = bf16[512,1728]{0,1:T(8,128)(2,1)} copy(bf16[512,1728]{1,0:T(8,128)(2,1)} %slice.106) | data formatting | bytes 3538944 | tf_op jit(solution)/shard_map/slice | solution.py:150
  102.1 2.4 %fusion.57 = (bf16[512,1,576]{0,2,1:T(8,128)(2,1)}, bf16[512,1,576]{0,2,1:T(8,128)(2,1)S(1)}, bf16[512,1,576]{0,2,1:T(8,128)(2,1)S(1)}) fusion(bf16[512,3,576]{0,2,1:T(8,128)(2,1)} %bitcast.62), kind=kLoop, calls=%fused_computation.105 | loop fusion | bytes 3538944 | tf_op jit(solution)/shard_map/slice | solution.py:48
  104.5 1.2 convert.40
  106.1 1.6 subtract_convert_fusion
  107.7 2.8 %fusion = (f32[9,512]{1,0:T(8,128)S(1)}, f32[9,512,1024]{2,1,0:T(8,128)S(1)}) fusion(pred[1024]{0:T(1024)(128)(4,1)S(1)} %iota_compare_fusion.3, bf16[1024,9,64]{0,2,1:T(8,128)(2,1)S(1)} %bitcast.65, bf16[512,9,32]{0,2,1:T(8,128)(2,1)S(1)} %get-tuple-element.17, bf16[512,9,32]{0,2,1:T(8,128)(2,1)S(1)} %get-tuple-element.18), kind=kOutput, calls=%fused_computation.3 | convolution fusion | flops 619310592 | bytes 20663296 | tf_op jit(solution)/shard_map/qhe,khe->hqk/dot_general | solution.py:52
  110.5 5.3 %fusion.3 = (f32[9,512]{1,0:T(8,128)S(1)}, f32[9,512,512]{1,2,0:T(8,128)}) fusion(pred[512,512]{0,1:T(8,128)(4,1)S(1)} %iota_compare_fusion, bf16[512,9,32]{0,2,1:T(8,128)(2,1)S(1)} %get-tuple-element.14, bf16[512,9,32]{0,2,1:T(8,128)(2,1)S(1)} %get-tuple-element.13, bf16[512,9,32]{0,2,1:T(8,128)(2,1)S(1)} %get-tuple-element.17, ...), kind=kOutput, calls=%fused_computation.9 | convolution fusion | flops 311422464 | bytes 10897408 | tf_op jit(solution)/shard_map/qhe,khe->hqk/dot_general | solution.py:56
  115.8 4.5 %fusion.1 = f32[9,512]{1,0:T(8,128)S(1)} fusion(f32[9,512,1024]{2,1,0:T(8,128)S(1)} %get-tuple-element.35, f32[9,512]{1,0:T(8,128)S(1)} %max.11, pred[1024]{0:T(1024)(128)(4,1)S(1)} %iota_compare_fusion.3), kind=kLoop, calls=%fused_computation.4 | loop fusion | flops 18869760 | bytes 18912256 | tf_op jit(solution)/shard_map/reduce_sum | solution.py:71
  120.4 5.6 %fusion.4 = f32[9,512]{1,0:T(8,128)S(1)} fusion(f32[9,512,512]{1,2,0:T(8,128)} %get-tuple-element.37, f32[9,512]{1,0:T(8,128)S(1)} %max.11, pred[512,512]{0,1:T(8,128)(4,1)S(1)} %iota_compare_fusion), kind=kLoop, calls=%fused_computation.10 | loop fusion | flops 9432576 | bytes 9736192 | tf_op jit(solution)/shard_map/reduce_sum | solution.py:71
  126.0 7.1 %fusion.16 = f32[512,9,64]{0,2,1:T(8,128)} fusion(bf16[1024,9,64]{0,2,1:T(8,128)(2,1)} %bitcast.69, f32[9,512,1024]{2,1,0:T(8,128)S(1)} %get-tuple-element.35, f32[9,512]{1,0:T(8,128)S(1)} %add.78, f32[9,512]{1,0:T(8,128)S(1)} %max.11, pred[1024]{0:T(1024)(128)(4,1)S(1)} %iota_compare_fusion.3), kind=kOutput, calls=%fused_computation.29 | convolution fusion | flops 627572736 | bytes 21271552 | tf_op jit(solution)/shard_map/hqk,khe->qhe/dot_general | solution.py:76
  133.1 6.0 %fusion.19 = bf16[512,9,64]{0,2,1:T(8,128)(2,1)S(1)} fusion(f32[512,9,64]{0,2,1:T(8,128)} %fusion.16, bf16[512,9,64]{0,2,1:T(8,128)(2,1)S(1)} %bitcast.70, f32[9,512,512]{1,2,0:T(8,128)} %get-tuple-element.37, f32[9,512]{1,0:T(8,128)S(1)} %add.78, f32[9,512]{1,0:T(8,128)S(1)} %max.11, pred[512,512]{0,1:T(8,128)(4,1)S(1)} %iota_compare_fusion), kind=kOutput, calls=%fused_computation.32 | convolution fusion | flops 314376192 | bytes 12095488 | tf_op jit(solution)/shard_map/hqk,khe->qhe/dot_general | solution.py:79
  139.1 3.5 %convolution_convert_fusion = bf16[520,2304]{1,0:T(8,128)(2,1)} fusion(bf16[576,2304]{1,0:T(8,128)(2,1)S(1)} %copy-done, bf16[8,576]{0,1:T(8,128)(2,1)S(1)} %copy-done.4, bf16[512,576]{0,1:T(8,128)(2,1)S(1)} %bitcast.72), kind=kOutput, calls=%fused_computation.24 | convolution fusion | flops 1382584320 | bytes 5649408 | tf_op jit(solution)/shard_map/dot_general | solution.py:169
  142.6 57.6 %all-reduce.2.cloned.1.call-done = bf16[520,2304]{1,0:T(8,128)(2,1)} async-done(((bf16[520,2304]{1,0:T(8,128)(2,1)}), bf16[520,2304]{1,0:T(8,128)(2,1)}) %all-reduce.2.cloned.1.call-update) | async-done | bytes 2396176 | tf_op jit(solution)/shard_map/psum | solution.py:170
  200.2 3.4 %fusion.5 = (f32[520]{0:T(1024)S(1)}, bf16[520,2304]{1,0:T(8,128)(2,1)S(1)}) fusion(bf16[520,2304]{1,0:T(8,128)(2,1)} %all-reduce.2.cloned.1.call-done, bf16[8,2304]{1,0:T(8,128)(2,1)S(1)} %copy-done.3, bf16[512,2304]{1,0:T(8,128)(2,1)} %param.11), kind=kLoop, calls=%fused_computation.16 | loop fusion | flops 11980280 | bytes 7190560 | tf_op jit(solution)/shard_map/reduce_sum | solution.py:15
  203.6 1.6 slice.122
  206.4 1.6 slice.124
  (61 shorter events, 6.9 us)
Async XLA Ops:
  7.2 131.9 %copy-start = (bf16[576,2304]{1,0:T(8,128)(2,1)S(1)}, bf16[576,2304]{1,0:T(8,128)(2,1)}, u32[]{:S(2)}) copy-start(bf16[576,2304]{1,0:T(8,128)(2,1)} %param.15) | copy-start | bytes 7962628
  7.2 193.0 %all-reduce.2.cloned.1.call-start = ((), (), s32[]{:S(2)}) async-start(), calls=%async_computation | async-start | bytes 4792320 | tf_op jit(solution)/shard_map/psum | solution.py:170
  8.8 12.5 %slice-start = ((s8[4718592]{0:T(1024)(128)(4,1)}), s8[4194304]{0:T(1024)(128)(4,1)S(1)}, s32[]{:S(2)}) async-start(s8[4718592]{0:T(1024)(128)(4,1)} %bitcast.63), calls=%async_computation.1 | async-start | bytes 8388608
  11.2 10.1 %slice-start.1 = ((s8[4718592]{0:T(1024)(128)(4,1)}), s8[524288]{0:T(1024)(128)(4,1)S(1)}, s32[]{:S(2)}) async-start(s8[4718592]{0:T(1024)(128)(4,1)} %bitcast.63), calls=%async_computation.2 | async-start | bytes 1048576
  21.3 35.1 %copy-start.6 = (s32[64]{0:T(128)S(1)}, s32[64]{0:T(128)}, u32[]{:S(2)}) copy-start(s32[64]{0:T(128)} %param.21) | copy-start | bytes 772
  105.6 2.1 copy-start.1
  126.0 7.1 %copy-start.2 = (bf16[512,1,576]{0,2,1:T(8,128)(2,1)S(1)}, bf16[512,1,576]{0,2,1:T(8,128)(2,1)}, u32[]{:S(2)}) copy-start(bf16[512,1,576]{0,2,1:T(8,128)(2,1)} %get-tuple-element.10) | copy-start | bytes 1769476
  133.1 6.0 %copy-start.4 = (bf16[8,576]{0,1:T(8,128)(2,1)S(1)}, bf16[8,576]{0,1:T(8,128)(2,1)}, u32[]{:S(2)}) copy-start(bf16[8,576]{0,1:T(8,128)(2,1)} %copy.27) | copy-start | bytes 27652
  139.1 61.1 %copy-start.3 = (bf16[8,2304]{1,0:T(8,128)(2,1)S(1)}, bf16[8,2304]{1,0:T(8,128)(2,1)}, u32[]{:S(2)}) copy-start(bf16[8,2304]{1,0:T(8,128)(2,1)} %param.12) | copy-start | bytes 110596
  142.6 63.2 %copy-start.5 = (f32[2304]{0:T(1024)S(1)}, f32[2304]{0:T(1024)}, u32[]{:S(2)}) copy-start(f32[2304]{0:T(1024)} %param.16) | copy-start | bytes 27652
Sparse Core Ops, SparseCore 0:
  142.8 57.4 all-reduce.1
where the time goes:
time: 216 us; the launch traced here: 215 us
  blocking collectives  63.1 us (29%)
  waiting for transfers between devices  57.6 us (27%)
  matrix products  38.1 us (18%)
  other arithmetic  22.4 us (10%)
  local copies, waits for them, and re-layouts  19.3 us (9%)
  between operations  15 us (7%)
    psum x1, waiting for transfers between devices, local(): lax.psum(partial_value.astype(jnp.bfloat16), 'tp').astype(jnp.float32)  57.6 us
    all_gather x1, blocking collectives, local(): arrived = lax.all_gather(decode_block, 'seq', axis=0, tiled=True)  32.5 us
    all_gather x1, blocking collectives, local(): shard_piece = lax.all_gather(slot_results, 'seq', axis=0, tiled=True)  30.5 us
    dot_general x1, matrix products, local(): jnp.dot(normed_in, qkv_weight.reshape(model_width, 3 * local_width), pref...  8.62 us
    dot_general x1, matrix products, prefill_attention(): jnp.einsum('hqk,khe->qhe', cache_weights, cache_values, preferred_element...  7.07 us
    dot_general x1, matrix products, prefill_attention(): jnp.einsum('hqk,khe->qhe', span_weights, new_values, preferred_element_ty...  6 us
    reduce_sum x2, other arithmetic, rms_norm(): jnp.mean(widened * widened, axis=-1, keepdims=True) + RMS_EPSILON  5.77 us
    reduce_sum x1, other arithmetic, prefill_attention(): jnp.sum(span_exp, axis=-1, keepdims=True)  5.61 us
  transfers between devices with their start and end apart: 1, of which 1 were waited for; matrix products, arithmetic and copies ran while one was open for 0% of the time, Pallas kernels for 0%

commit v1 on v0

--- a/solution.py
+++ b/solution.py
@@ -161,7 +161,12 @@
         prefill_block, prefill_cache[0], prefill_offsets[0], head_count
     )
     my_slots = lax.dynamic_slice_in_dim(request_slot, seq_rank * decode_rows, decode_rows)
-    shard_piece = lax.all_gather(slot_results, "seq", axis=0, tiled=True)
+    ring = [slot_results]
+    for hop in range(7):
+        ring.append(lax.ppermute(ring[-1], "seq", [(dev, (dev + 1) % 8) for dev in range(8)]))
+    shard_piece = jnp.roll(
+        jnp.concatenate(ring[::-1], axis=0), (lax.axis_index("seq") + 1) * ring[0].shape[0], axis=0
+    )
     slot_ids = jnp.arange(shard_piece.shape[0], dtype=jnp.int32)
     picker = (my_slots[:, None] == slot_ids[None, :]).astype(jnp.bfloat16)
     returned = jnp.dot(picker, shard_piece, preferred_element_type=jnp.float32).astype(jnp.bfloat16)

time: 216 us -> 199 us (0.921)
  blocking collectives: 63.1 us -> 32.5 us
  waiting for transfers between devices: 57.6 us -> 68.8 us
  local copies, waits for them, and re-layouts: 19.3 us -> 23.8 us
  matrix products: 38.1 us -> 35.8 us
  starting transfers between devices: 0.04 us -> 2.28 us
    all_gather x1 -> x0, blocking collectives: 30.5 us -> none  [local(): shard_piece = lax.all_gather(slot_results, 'seq', axis=0, tiled=True)]
    ppermute x0 -> x7, waiting for transfers between devices: none -> 9.78 us  [local(): lax.ppermute(ring[-1], 'seq', [(dev, (dev + 1) % 8) for dev in range(8)])]
    dot_general x1, matrix products: 8.62 us -> 4.69 us  [local(): jnp.dot(normed_in, qkv_weight.reshape(model_width, 3 * local_width), pref...]
    slice x1, local copies, waits for them, and re-layouts: 2.49 us -> 5.35 us  [decode_attention(): cache_block[:, 0].reshape(slot_count, cache_len, head_count, HEAD)]
    unnamed x18 -> x37, local copies, waits for them, and re-layouts: 0.05 us -> 2.62 us
    ppermute x0 -> x7, starting transfers between devices: none -> 2.25 us  [local(): lax.ppermute(ring[-1], 'seq', [(dev, (dev + 1) % 8) for dev in range(8)])]
  transfers between devices with their start and end apart: 1 -> 8, of which waited for: 1 -> 5; matrix products, arithmetic and copies ran while one was open for 0% -> 23% of each run, Pallas kernels for 0% -> 0%
where the time goes in v1:
time: 199 us
  waiting for transfers between devices  68.8 us (35%)
  matrix products  35.8 us (18%)
  blocking collectives  32.5 us (16%)
  local copies, waits for them, and re-layouts  23.8 us (12%)
  other arithmetic  20.5 us (10%)
  between operations  15 us (8%)
  starting transfers between devices  2.28 us (1%)
    psum x1, waiting for transfers between devices, local(): lax.psum(partial_value.astype(jnp.bfloat16), 'tp').astype(jnp.float32)  59 us
    all_gather x1, blocking collectives, local(): arrived = lax.all_gather(decode_block, 'seq', axis=0, tiled=True)  32.5 us
    ppermute x7, waiting for transfers between devices, local(): lax.ppermute(ring[-1], 'seq', [(dev, (dev + 1) % 8) for dev in range(8)])  9.78 us
    dot_general x1, matrix products, prefill_attention(): jnp.einsum('hqk,khe->qhe', cache_weights, cache_values, preferred_element...  7.08 us
    slice x2, local copies, waits for them, and re-layouts, local(): prefill_block = projected[:span_rows]  6.66 us
    dot_general x1, matrix products, prefill_attention(): jnp.einsum('hqk,khe->qhe', span_weights, new_values, preferred_element_ty...  6.54 us
    reduce_sum x1, other arithmetic, prefill_attention(): jnp.sum(span_exp, axis=-1, keepdims=True)  5.62 us
    slice x1, local copies, waits for them, and re-layouts, decode_attention(): cache_block[:, 0].reshape(slot_count, cache_len, head_count, HEAD)  5.35 us
  transfers between devices with their start and end apart: 8, of which 5 were waited for; matrix products, arithmetic and copies ran while one was open for 23% of the time, Pallas kernels for 0%

profile of v1, /device:TPU:0, one launch (start us, length us, event | category | flops | bytes accessed | tf_op | source)
XLA Modules:
  0.0 198.7 jit_solution(11081245335947935081)
XLA Ops:
  8.8 5.3 %fusion.57 = (bf16[8,1,256,576]{2,3,1,0:T(8,128)(2,1)}, bf16[8,1,256,576]{2,3,1,0:T(8,128)(2,1)}) fusion(bf16[8,2,256,576]{2,3,1,0:T(8,128)(2,1)} %param.19), kind=kLoop, calls=%fused_computation.121 | loop fusion | bytes 9437184 | tf_op jit(solution)/shard_map/slice | solution.py:97
  15.9 4.7 %convolution_convert_fusion.1 = bf16[520,1728]{1,0:T(8,128)(2,1)S(1)} fusion(bf16[2304,1728]{0,1:T(8,128)(2,1)S(1)} %bitcast.68, f32[2304]{0:T(1024)S(1)} %copy-done.10, f32[520]{0:T(1024)S(1)} %add_rsqrt_fusion.1, bf16[8,2304]{1,0:T(8,128)(2,1)S(1)} %copy-done.6, bf16[512,2304]{1,0:T(8,128)(2,1)S(1)} %copy-done.1), kind=kOutput, calls=%fused_computation.25 | convolution fusion | flops 4149849600 | bytes 12167200 | tf_op jit(solution)/shard_map/dot_general | solution.py:144
  22.0 32.5 %all_gather.3 = bf16[64,3,576]{2,0,1:T(8,128)(2,1)S(1)} all-gather(bf16[8,3,576]{2,0,1:T(8,128)(2,1)S(1)} %copy.25), channel_id=1, replica_groups=mesh['seq'=8,'tp'=4] {'seq'}, dimensions={0}, use_global_device_ids=true | all-gather | bytes 248832 | tf_op jit(solution)/shard_map/all_gather | solution.py:154
  55.5 2.1 %fusion.36 = f32[8,9,1,256]{3,2,1,0:T(1,128)S(1)} fusion(bf16[8,256,9,64]{1,3,2,0:T(8,128)(2,1)} %bitcast.60, bf16[8,9,64,1]{2,1,0,3:T(8,128)(2,1)S(1)} %fusion.39), kind=kOutput, calls=%fused_computation.68 | convolution fusion | flops 2359296 | bytes 2442240 | tf_op jit(solution)/shard_map/she,skhe->shk/dot_general | solution.py:100
  58.1 2.4 %fusion.30 = f32[8,9,1,64]{3,2,1,0:T(1,128)S(1)} fusion(bf16[8,256,9,64]{1,3,2,0:T(8,128)(2,1)} %bitcast.65, bf16[8,9,256,1]{2,0,1,3:T(8,128)(2,1)S(1)} %fusion.38), kind=kOutput, calls=%fused_computation.54 | convolution fusion | flops 2359296 | bytes 2414592 | tf_op jit(solution)/shard_map/shk,skhe->she/dot_general | solution.py:115
  60.7 1.5 collective-permute-start
  62.2 2.8 %slice.106 = bf16[512,1728]{1,0:T(8,128)(2,1)} slice(bf16[520,1728]{1,0:T(8,128)(2,1)} %copy-done.4), slice={[0:512], [0:1728]} | slice | bytes 3538944 | tf_op jit(solution)/shard_map/slice | solution.py:150
  65.1 1.6 fusion.58
  67.4 3.8 %copy.23 = bf16[512,1728]{0,1:T(8,128)(2,1)} copy(bf16[512,1728]{1,0:T(8,128)(2,1)} %slice.106) | data formatting | bytes 3538944 | tf_op jit(solution)/shard_map/slice | solution.py:150
  71.2 2.4 %fusion.59 = (bf16[512,1,576]{0,2,1:T(8,128)(2,1)}, bf16[512,1,576]{0,2,1:T(8,128)(2,1)S(1)}, bf16[512,1,576]{0,2,1:T(8,128)(2,1)S(1)}) fusion(bf16[512,3,576]{0,2,1:T(8,128)(2,1)} %bitcast.61), kind=kLoop, calls=%fused_computation.123 | loop fusion | bytes 3538944 | tf_op jit(solution)/shard_map/slice | solution.py:48
  75.2 1.6 subtract_convert_fusion
  76.8 2.8 %fusion = (f32[9,512]{1,0:T(8,128)S(1)}, f32[9,512,1024]{2,1,0:T(8,128)S(1)}) fusion(pred[1024]{0:T(1024)(128)(4,1)S(1)} %iota_compare_fusion.3, bf16[1024,9,64]{0,2,1:T(8,128)(2,1)S(1)} %bitcast.62, bf16[512,9,32]{0,2,1:T(8,128)(2,1)S(1)} %get-tuple-element.17, bf16[512,9,32]{0,2,1:T(8,128)(2,1)S(1)} %get-tuple-element.18), kind=kOutput, calls=%fused_computation.3 | convolution fusion | flops 619310592 | bytes 20663296 | tf_op jit(solution)/shard_map/qhe,khe->hqk/dot_general | solution.py:52
  79.9 6.1 %collective-permute-done.1 = bf16[8,576]{1,0:T(8,128)(2,1)S(1)} collective-permute-done((bf16[8,576]{1,0:T(8,128)(2,1)S(1)}, bf16[8,576]{1,0:T(8,128)(2,1)S(1)}, u32[]{:S(2)}, u32[]{:S(2)}) %collective-permute-start.1) | collective-permute-done | bytes 9248 | tf_op jit(solution)/shard_map/ppermute | solution.py:166
  86.0 5.3 %fusion.3 = (f32[9,512]{1,0:T(8,128)S(1)}, f32[9,512,512]{1,2,0:T(8,128)}) fusion(pred[512,512]{0,1:T(8,128)(4,1)S(1)} %iota_compare_fusion, bf16[512,9,32]{0,2,1:T(8,128)(2,1)S(1)} %get-tuple-element.14, bf16[512,9,32]{0,2,1:T(8,128)(2,1)S(1)} %get-tuple-element.13, bf16[512,9,32]{0,2,1:T(8,128)(2,1)S(1)} %get-tuple-element.17, ...), kind=kOutput, calls=%fused_computation.9 | convolution fusion | flops 311422464 | bytes 10897408 | tf_op jit(solution)/shard_map/qhe,khe->hqk/dot_general | solution.py:56
  92.4 4.5 %fusion.1 = f32[9,512]{1,0:T(8,128)S(1)} fusion(f32[9,512,1024]{2,1,0:T(8,128)S(1)} %get-tuple-element.35, f32[9,512]{1,0:T(8,128)S(1)} %max.11, pred[1024]{0:T(1024)(128)(4,1)S(1)} %iota_compare_fusion.3), kind=kLoop, calls=%fused_computation.4 | loop fusion | flops 18869760 | bytes 18912256 | tf_op jit(solution)/shard_map/reduce_sum | solution.py:71
  96.9 1.8 collective-permute-done.3
  98.8 5.6 %fusion.4 = f32[9,512]{1,0:T(8,128)S(1)} fusion(f32[9,512,512]{1,2,0:T(8,128)} %get-tuple-element.37, f32[9,512]{1,0:T(8,128)S(1)} %max.11, pred[512,512]{0,1:T(8,128)(4,1)S(1)} %iota_compare_fusion), kind=kLoop, calls=%fused_computation.10 | loop fusion | flops 9432576 | bytes 9736192 | tf_op jit(solution)/shard_map/reduce_sum | solution.py:71
  105.1 7.1 %fusion.16 = f32[512,9,64]{0,2,1:T(8,128)} fusion(bf16[1024,9,64]{0,2,1:T(8,128)(2,1)} %bitcast.66, f32[9,512,1024]{2,1,0:T(8,128)S(1)} %get-tuple-element.35, f32[9,512]{1,0:T(8,128)S(1)} %add.91, f32[9,512]{1,0:T(8,128)S(1)} %max.11, pred[1024]{0:T(1024)(128)(4,1)S(1)} %iota_compare_fusion.3), kind=kOutput, calls=%fused_computation.29 | convolution fusion | flops 627572736 | bytes 21271552 | tf_op jit(solution)/shard_map/hqk,khe->qhe/dot_general | solution.py:76
  112.7 6.5 %fusion.19 = bf16[512,9,64]{0,2,1:T(8,128)(2,1)} fusion(f32[512,9,64]{0,2,1:T(8,128)} %fusion.16, bf16[512,9,64]{0,2,1:T(8,128)(2,1)S(1)} %bitcast.67, f32[9,512,512]{1,2,0:T(8,128)} %get-tuple-element.37, f32[9,512]{1,0:T(8,128)S(1)} %add.91, f32[9,512]{1,0:T(8,128)S(1)} %max.11, pred[512,512]{0,1:T(8,128)(4,1)S(1)} %iota_compare_fusion), kind=kOutput, calls=%fused_computation.32 | convolution fusion | flops 314376192 | bytes 12095488 | tf_op jit(solution)/shard_map/hqk,khe->qhe/dot_general | solution.py:79
  119.9 4.6 %convolution_convert_fusion = bf16[520,2304]{1,0:T(8,128)(2,1)} fusion(bf16[576,2304]{1,0:T(8,128)(2,1)S(1)} %copy-done, bf16[8,576]{0,1:T(8,128)(2,1)S(1)} %copy.27, bf16[512,576]{0,1:T(8,128)(2,1)} %bitcast.69), kind=kOutput, calls=%fused_computation.24 | convolution fusion | flops 1382584320 | bytes 5649408 | tf_op jit(solution)/shard_map/dot_general | solution.py:174
  124.5 59.0 %all-reduce.2.cloned.1.call-done = bf16[520,2304]{1,0:T(8,128)(2,1)} async-done(((bf16[520,2304]{1,0:T(8,128)(2,1)}), bf16[520,2304]{1,0:T(8,128)(2,1)}) %all-reduce.2.cloned.1.call-update) | async-done | bytes 2396176 | tf_op jit(solution)/shard_map/psum | solution.py:175
  183.5 3.4 %fusion.5 = (f32[520]{0:T(1024)S(1)}, bf16[520,2304]{1,0:T(8,128)(2,1)S(1)}) fusion(bf16[520,2304]{1,0:T(8,128)(2,1)} %all-reduce.2.cloned.1.call-done, bf16[8,2304]{1,0:T(8,128)(2,1)S(1)} %copy-done.6, bf16[512,2304]{1,0:T(8,128)(2,1)} %param.11), kind=kLoop, calls=%fused_computation.16 | loop fusion | flops 11980280 | bytes 7190560 | tf_op jit(solution)/shard_map/reduce_sum | solution.py:15
  186.9 1.6 slice.122
  189.7 1.6 slice.124
  (93 shorter events, 13.1 us)
Async XLA Ops:
  7.2 112.7 %copy-start = (bf16[576,2304]{1,0:T(8,128)(2,1)S(1)}, bf16[576,2304]{1,0:T(8,128)(2,1)}, u32[]{:S(2)}) copy-start(bf16[576,2304]{1,0:T(8,128)(2,1)} %param.15) | copy-start | bytes 7962628
  7.2 176.3 %all-reduce.2.cloned.1.call-start = ((), (), s32[]{:S(2)}) async-start(), calls=%async_computation | async-start | bytes 4792320 | tf_op jit(solution)/shard_map/psum | solution.py:175
  8.8 5.4 %copy-start.1 = (bf16[512,2304]{1,0:T(8,128)(2,1)S(1)}, bf16[512,2304]{1,0:T(8,128)(2,1)}, u32[]{:S(2)}) copy-start(bf16[512,2304]{1,0:T(8,128)(2,1)} %param.11) | copy-start | bytes 7077892
  8.8 5.4 %copy-start.6 = (bf16[8,2304]{1,0:T(8,128)(2,1)S(1)}, bf16[8,2304]{1,0:T(8,128)(2,1)}, u32[]{:S(2)}) copy-start(bf16[8,2304]{1,0:T(8,128)(2,1)} %param.12) | copy-start | bytes 110596
  8.8 7.1 %copy-start.9 = (bf16[2304,3,576]{0,2,1:T(8,128)(2,1)S(1)}, bf16[2304,3,576]{0,2,1:T(8,128)(2,1)}, u32[]{:S(2)}) copy-start(bf16[2304,3,576]{0,2,1:T(8,128)(2,1)} %param.14) | copy-start | bytes 23887876
  8.8 7.1 %copy-start.10 = (f32[2304]{0:T(1024)S(1)}, f32[2304]{0:T(1024)}, u32[]{:S(2)}) copy-start(f32[2304]{0:T(1024)} %param.13) | copy-start | bytes 27652
  15.9 38.6 %copy-start.8 = (s32[64]{0:T(128)S(1)}, s32[64]{0:T(128)}, u32[]{:S(2)}) copy-start(s32[64]{0:T(128)} %param.21) | copy-start | bytes 772
  20.6 1.3 copy-start.4
  60.7 4.4 %copy-start.3 = (bf16[1,2,1024,576]{2,3,1,0:T(8,128)(2,1)S(1)}, bf16[1,2,1024,576]{2,3,1,0:T(8,128)(2,1)}, u32[]{:S(2)}) copy-start(bf16[1,2,1024,576]{2,3,1,0:T(8,128)(2,1)} %param.17) | copy-start | bytes 7077892
  60.7 18.9 %collective-permute-start = (bf16[8,576]{1,0:T(8,128)(2,1)S(1)}, bf16[8,576]{1,0:T(8,128)(2,1)S(1)}, u32[]{:S(2)}, u32[]{:S(2)}) collective-permute-start(bf16[8,576]{1,0:T(8,128)(2,1)S(1)} %convert_element_type.124), channel_id=1, source_target_pairs={{0,4},{4,8},{8,12},{12,16},{16,20},{20,24},{24,28},{28,0},{1,5},{5... | collective-permute-start | bytes 27656 | tf_op jit(solution)/shard_map/ppermute | solution.py:166
  74.7 2.1 %copy-start.2 = (bf16[1,1,1024,576]{2,3,1,0:T(8,128)(2,1)S(1)}, bf16[1,1,1024,576]{2,3,1,0:T(8,128)(2,1)}, u32[]{:S(2)}) copy-start(bf16[1,1,1024,576]{2,3,1,0:T(8,128)(2,1)} %get-tuple-element.8) | copy-start | bytes 3538948
  79.6 6.4 %collective-permute-start.1 = (bf16[8,576]{1,0:T(8,128)(2,1)S(1)}, bf16[8,576]{1,0:T(8,128)(2,1)S(1)}, u32[]{:S(2)}, u32[]{:S(2)}) collective-permute-start(bf16[8,576]{1,0:T(8,128)(2,1)S(1)} %collective-permute-done), channel_id=1, source_target_pairs={{0,4},{4,8},{8,12},{12,16},{16,20},{20,24},{24,28},{28,0},{1,5},{5... | collective-permute-start | bytes 27656 | tf_op jit(solution)/shard_map/ppermute | solution.py:166
  86.0 6.4 %collective-permute-start.2 = (bf16[8,576]{1,0:T(8,128)(2,1)S(1)}, bf16[8,576]{1,0:T(8,128)(2,1)S(1)}, u32[]{:S(2)}, u32[]{:S(2)}) collective-permute-start(bf16[8,576]{1,0:T(8,128)(2,1)S(1)} %collective-permute-done.1), channel_id=1, source_target_pairs={{0,4},{4,8},{8,12},{12,16},{16,20},{20,24},{24,28},{28,0},{1,5},{5... | collective-permute-start | bytes 27656 | tf_op jit(solution)/shard_map/ppermute | solution.py:166
  92.4 6.4 %collective-permute-start.3 = (bf16[8,576]{1,0:T(8,128)(2,1)S(1)}, bf16[8,576]{1,0:T(8,128)(2,1)S(1)}, u32[]{:S(2)}, u32[]{:S(2)}) collective-permute-start(bf16[8,576]{1,0:T(8,128)(2,1)S(1)} %collective-permute-done.2), channel_id=1, source_target_pairs={{0,4},{4,8},{8,12},{12,16},{16,20},{20,24},{24,28},{28,0},{1,5},{5... | collective-permute-start | bytes 27656 | tf_op jit(solution)/shard_map/ppermute | solution.py:166
  98.8 6.4 %collective-permute-start.4 = (bf16[8,576]{1,0:T(8,128)(2,1)S(1)}, bf16[8,576]{1,0:T(8,128)(2,1)S(1)}, u32[]{:S(2)}, u32[]{:S(2)}) collective-permute-start(bf16[8,576]{1,0:T(8,128)(2,1)S(1)} %collective-permute-done.3), channel_id=1, source_target_pairs={{0,4},{4,8},{8,12},{12,16},{16,20},{20,24},{24,28},{28,0},{1,5},{5... | collective-permute-start | bytes 27656 | tf_op jit(solution)/shard_map/ppermute | solution.py:166
  105.1 7.1 %collective-permute-start.5 = (bf16[8,576]{1,0:T(8,128)(2,1)S(1)}, bf16[8,576]{1,0:T(8,128)(2,1)S(1)}, u32[]{:S(2)}, u32[]{:S(2)}) collective-permute-start(bf16[8,576]{1,0:T(8,128)(2,1)S(1)} %collective-permute-done.4), channel_id=1, source_target_pairs={{0,4},{4,8},{8,12},{12,16},{16,20},{20,24},{24,28},{28,0},{1,5},{5... | collective-permute-start | bytes 27656 | tf_op jit(solution)/shard_map/ppermute | solution.py:166
  105.1 7.6 %copy-start.5 = (bf16[512,1,576]{0,2,1:T(8,128)(2,1)S(1)}, bf16[512,1,576]{0,2,1:T(8,128)(2,1)}, u32[]{:S(2)}) copy-start(bf16[512,1,576]{0,2,1:T(8,128)(2,1)} %get-tuple-element.10) | copy-start | bytes 1769476
  112.2 7.1 %collective-permute-start.6 = (bf16[8,576]{1,0:T(8,128)(2,1)S(1)}, bf16[8,576]{1,0:T(8,128)(2,1)S(1)}, u32[]{:S(2)}, u32[]{:S(2)}) collective-permute-start(bf16[8,576]{1,0:T(8,128)(2,1)S(1)} %collective-permute-done.5), channel_id=1, source_target_pairs={{0,4},{4,8},{8,12},{12,16},{16,20},{20,24},{24,28},{28,0},{1,5},{5... | collective-permute-start | bytes 27656 | tf_op jit(solution)/shard_map/ppermute | solution.py:166
  124.5 64.6 %copy-start.7 = (f32[2304]{0:T(1024)S(1)}, f32[2304]{0:T(1024)}, u32[]{:S(2)}) copy-start(f32[2304]{0:T(1024)} %param.16) | copy-start | bytes 27652
Sparse Core Ops, SparseCore 0:
  124.6 58.8 all-reduce.1
